TPU v7x, 512 devices: a whole 4x8x8 slice. The times are simulated.
512 devices in a mesh: dp: 4 (over x), ctx: 16 (over y, core), tensor: 8 (over z).
Axes of the slice: x: 4, y: 8, z: 8, core: 2. Of those that a mesh axis runs over, the one named last changes fastest.
Arguments:
- tokens: bfloat16 [8192, 8192], P(('dp', 'tensor'), 'ctx'), parts along dimension 0, may hold values from -6 to 6
- queries: bfloat16 [8192, 8192], P(('dp', 'ctx'), 'tensor'), parts along dimension 0, may hold values from -100 to 100
- key_value_weight: bfloat16 [8192, 2048], P('ctx', 'tensor'), may hold values from -0.0625 to 0.0625
- out_weight: bfloat16 [8192, 8192], P('tensor', 'ctx'), may hold values from -0.0625 to 0.0625
- doc_lengths: int32 [32], P('dp'), parts along dimension 0, may hold values from 1 to 1024, 2048 in all
- block_order: int32 [128], P('dp'), parts along dimension 0, may hold values from 0 to 31, each once
Outputs:
- mixed: bfloat16 [8192, 8192], P(('dp', 'tensor'), 'ctx'), parts along dimension 0
There are 4 independent parts, one for each index of `dp`. A program takes and returns all parts, laid end to end along the dimension named above; an argument that names none is the same for every part. Nothing has to cross between parts.
Inputs may be any that keep to these rules, and one draw needn't show every extreme that they name: `doc_lengths`: the lengths add up to 2048. `block_order`: each of 0 to 31 once.
All inputs are finite; a program needn't handle non-finite values.
Results may differ from a plain program's by a relative error of at most 0.014.
Values may be sent and summed in bfloat16 or wider, within the bound.
No kernel may reach another device: no remote copies, remote signals or barrier semaphores. Data moves between devices by JAX's collectives and lax.ppermute only.
A program may use at most 64 MiB of HBM per device.

v0:
```python
import math
import jax
import jax.numpy as jnp
from jax import lax
from jax.sharding import PartitionSpec as P

HEAD_WIDTH = 128


def doc_index(positions, doc_ends):
    return jnp.sum((doc_ends[None, :] <= positions[:, None]).astype(jnp.int32), axis=1)


def make_attend(query_groups, query_pos, query_doc, doc_ends):
    scale = 1.0 / jnp.sqrt(jnp.float32(HEAD_WIDTH))

    def attend(running, kv_piece, first_row):
        key_count = kv_piece.shape[0]
        key_pos = first_row + jnp.arange(key_count, dtype=jnp.int32)
        key_doc = doc_index(key_pos, doc_ends)
        allowed = (query_doc[:, None] == key_doc[None, :]) & (
            key_pos[None, :] <= query_pos[:, None]
        )

        def update(state_in):
            top_score, total, weighted = state_in
            split_kv = kv_piece.reshape(key_count, query_groups.shape[1], 2, HEAD_WIDTH)
            keys_now = split_kv[:, :, 0, :]
            values_now = split_kv[:, :, 1, :]
            scores = (
                jnp.einsum(
                    "tkgd,nkd->tkgn", query_groups, keys_now, preferred_element_type=jnp.float32
                )
                * scale
            )
            visible = allowed[:, None, None, :]
            piece_top = jnp.max(jnp.where(visible, scores, jnp.float32(-1e30)), axis=-1)
            new_top = jnp.maximum(top_score, piece_top)
            probs = jnp.where(visible, jnp.exp(scores - new_top[..., None]), jnp.float32(0.0))
            rescale = jnp.exp(top_score - new_top)
            total = total * rescale + jnp.sum(probs, axis=-1)
            weighted = weighted * rescale[..., None] + jnp.einsum(
                "tkgn,nkd->tkgd",
                probs.astype(jnp.bfloat16),
                values_now,
                preferred_element_type=jnp.float32,
            )
            return (new_top, total, weighted)

        def unchanged(state_in):
            return state_in

        return lax.cond(jnp.any(allowed), update, unchanged, running)

    return attend


def local(tokens, queries, key_value_weight, out_weight, doc_lengths, block_order):
    ctx_count = lax.axis_size("ctx")
    ctx_rank = lax.axis_index("ctx")
    local_rows = queries.shape[0]
    seq_rows = local_rows * ctx_count
    half_rows = local_rows // 2
    doc_ends = jnp.cumsum(doc_lengths)
    own_blocks = lax.dynamic_slice_in_dim(block_order, 2 * ctx_rank, 2)
    query_pos = jnp.repeat(
        own_blocks, half_rows, total_repeat_length=local_rows
    ) * half_rows + jnp.tile(jnp.arange(half_rows, dtype=jnp.int32), 2)
    query_doc = doc_index(query_pos, doc_ends)
    heads_width = queries.shape[1]
    kv_heads = key_value_weight.shape[1] // (2 * HEAD_WIDTH)
    queries_per_group = heads_width // HEAD_WIDTH // kv_heads
    query_groups = queries.reshape(local_rows, kv_heads, queries_per_group, HEAD_WIDTH)
    attend = make_attend(query_groups, query_pos, query_doc, doc_ends)
    initial = (
        jnp.full((local_rows, kv_heads, queries_per_group), -1e30, jnp.float32),
        jnp.zeros((local_rows, kv_heads, queries_per_group), jnp.float32),
        jnp.zeros((local_rows, kv_heads, queries_per_group, HEAD_WIDTH), jnp.float32),
    )
    partial_kv = jnp.dot(
        lax.all_gather(tokens, "tensor", axis=0, tiled=True),
        key_value_weight,
        preferred_element_type=jnp.float32,
    )
    whole_kv = lax.psum(partial_kv, "ctx").astype(jnp.bfloat16)
    key_step = math.gcd(seq_rows, 512)

    def visit(key_block, running):
        kv_piece = lax.dynamic_slice_in_dim(whole_kv, key_block * key_step, key_step, 0)
        return attend(running, kv_piece, key_block * key_step)

    result = lax.fori_loop(0, seq_rows // key_step, visit, initial)
    top_score, total, weighted = result
    attn = (weighted / total[..., None]).astype(jnp.bfloat16).reshape(local_rows, heads_width)
    partial_out = jnp.dot(
        lax.all_gather(attn, "ctx", axis=0, tiled=True),
        out_weight,
        preferred_element_type=jnp.float32,
    )
    mixed = lax.psum_scatter(
        partial_out.astype(jnp.bfloat16), "tensor", scatter_dimension=0, tiled=True
    )
    return mixed


def solution(mesh):
    in_specs = (
        P(("dp", "tensor"), "ctx"),
        P(("dp", "ctx"), "tensor"),
        P("ctx", "tensor"),
        P("tensor", "ctx"),
        P("dp"),
        P("dp"),
    )
    out_specs = P(("dp", "tensor"), "ctx")
    return jax.shard_map(local, mesh=mesh, in_specs=in_specs, out_specs=out_specs, check_vma=False)
```

profile of v0, /device:TPU:8, one launch (start us, length us, event | category | flops | bytes accessed | tf_op | source)
XLA Modules:
  0.0 245.9 jit_solution(3208315371400769322)
XLA Ops:
  6.5 0.7 all-gather.3.cloned.1.call-update
  7.3 0.8 reduce-window.10
  8.2 1.1 copy.16
  9.6 0.7 dynamic_slice.14
  10.9 1.9 fusion.19
  12.8 45.1 %all-gather.3.cloned.1.call-done = bf16[2048,512]{1,0:T(8,128)(2,1)} async-done(((bf16[256,512]{1,0:T(8,128)(2,1)}), bf16[2048,512]{1,0:T(8,128)(2,1)}) %all-gather.3.cloned.1.call-update) | async-done | bytes 2097168 | tf_op jit(solution)/shard_map/all_gather | solution.py:81
  58.0 2.3 fusion.22
  60.3 55.5 %all-reduce.1 = bf16[2048,256]{1,0:T(8,128)(2,1)} all-reduce(f32[2048,256]{1,0:T(8,128)S(1)} %fusion.22), channel_id=1, replica_groups=mesh['dp'=4,'ctx'=16,'tensor'=8] {'ctx'}, use_global_device_ids=true, to_apply=%region_0.0 | all-reduce | flops 524288 | bytes 3145728 | tf_op jit(solution)/shard_map/psum | solution.py:85
  115.8 1.5 copy.17
  117.4 15.2 %while.19 = (s32[]{:T(128)}, f32[128,1,8]{0,2,1:T(8,128)S(1)}, f32[128,1,8]{0,2,1:T(8,128)S(1)}, f32[128,1,8,128]{0,3,2,1:T(8,128)S(1)}, s32[128]{0:T(128)S(1)},...) while((s32[]{:T(128)}, f32[128,1,8]{0,2,1:T(8,128)S(1)}, ...), condition=%wide.region_10.11_spmd.clone, body=%wide.region_3.10_spmd.clone.sunk | while | flops 274742656 | bytes 8730577 | solution.py:92
  117.5 1.2 multiply_add_fusion.2
  118.8 0.9 fusion.28
  120.3 1.7 conditional.3
  122.1 1.2 multiply_add_fusion.2
  123.4 0.9 fusion.28
  125.1 1.2 multiply_add_fusion.2
  126.4 0.9 fusion.28
  128.0 1.2 multiply_add_fusion.2
  129.4 0.9 fusion.28
  130.9 1.7 conditional.3
  132.6 0.8 divide_convert_fusion
  133.4 54.3 %all-gather.5.cloned.1.call-done = bf16[2048,1024]{0,1:T(8,128)(2,1)} async-done(((bf16[128,1024]{0,1:T(8,128)(2,1)}), bf16[2048,1024]{0,1:T(8,128)(2,1)}) %all-gather.5.cloned.1.call-update) | async-done | bytes 4194320 | tf_op jit(solution)/shard_map/all_gather | solution.py:96
  187.7 5.9 %convolution_convert_fusion = bf16[2048,512]{1,0:T(8,128)(2,1)} fusion(bf16[2048,1024]{0,1:T(8,128)(2,1)} %all-gather.5.cloned.1.call-done, bf16[1024,512]{1,0:T(8,128)(2,1)S(1)} %copy-done), kind=kOutput, calls=%fused_computation.30 | convolution fusion | flops 2148532224 | bytes 7340032 | tf_op jit(solution)/shard_map/dot_general | solution.py:95
  193.6 45.8 %reduce-scatter.2.cloned.1.call-done = bf16[256,512]{1,0:T(8,128)(2,1)} async-done(((bf16[2048,512]{1,0:T(8,128)(2,1)}), bf16[256,512]{1,0:T(8,128)(2,1)}) %reduce-scatter.2.cloned.1.call-update) | async-done | bytes 262160 | tf_op jit(solution)/shard_map/reduce_scatter | solution.py:100
  (49 shorter events, 5.1 us)
Async XLA Ops:
  6.5 181.1 %copy-start = (bf16[1024,512]{1,0:T(8,128)(2,1)S(1)}, bf16[1024,512]{1,0:T(8,128)(2,1)}, u32[]{:S(2)}) copy-start(bf16[1024,512]{1,0:T(8,128)(2,1)} %param.15) | copy-start | bytes 3145732
  6.5 51.5 %all-gather.3.cloned.1.call-start = ((), (), s32[]{:S(2)}) async-start(), calls=%async_computation.1 | async-start | bytes 2359296 | tf_op jit(solution)/shard_map/all_gather | solution.py:81
  7.3 180.4 %all-gather.5.cloned.1.call-start = ((), (), s32[]{:S(2)}) async-start(), calls=%async_computation.2 | async-start | bytes 4456448 | tf_op jit(solution)/shard_map/all_gather | solution.py:96
  115.8 1.6 copy-start.1
  133.3 106.0 %reduce-scatter.2.cloned.1.call-start = ((), (), s32[]{:S(2)}) async-start(), calls=%async_computation.3 | async-start | bytes 2359296 | tf_op jit(solution)/shard_map/reduce_scatter | solution.py:100
Sparse Core Ops, SparseCore 0:
  9.4 48.5 all-gather.2
  133.5 54.1 all-gather.4
  193.7 45.6 reduce-scatter.1
where the time goes:
time: 246 us
  waiting for transfers between devices  146 us (59%)
  blocking collectives  55.5 us (23%)
  other arithmetic  13.2 us (5%)
  between operations  13.2 us (5%)
  matrix products  10.4 us (4%)
  local copies, waits for them, and re-layouts  4.66 us (2%)
  loops' own time  2.91 us (1%)
    psum x1, blocking collectives, local(): whole_kv = lax.psum(partial_kv, 'ctx').astype(jnp.bfloat16)  55.5 us
    all_gather x1, waiting for transfers between devices, local(): lax.all_gather(attn, 'ctx', axis=0, tiled=True)  54.3 us
    reduce_scatter x1, waiting for transfers between devices, local(): lax.psum_scatter(partial_out.astype(jnp.bfloat16), 'tensor', scatter_dime...  45.8 us
    all_gather x1, waiting for transfers between devices, local(): lax.all_gather(tokens, 'tensor', axis=0, tiled=True)  45.1 us
    add x5, other arithmetic, local(): jnp.repeat(own_blocks, half_rows, total_repeat_length=local_rows)  6.79 us
    dot_general x1, matrix products, local(): jnp.dot(lax.all_gather(attn, 'ctx', axis=0, tiled=True), out_weight, pref...  5.9 us
  transfers between devices with their start and end apart: 3, of which 3 were waited for; matrix products, arithmetic and copies ran while one was open for 2% of the time, Pallas kernels for 0%

commit v1 on v0

--- a/solution.py
+++ b/solution.py
@@ -82,7 +82,7 @@
         key_value_weight,
         preferred_element_type=jnp.float32,
     )
-    whole_kv = lax.psum(partial_kv, "ctx").astype(jnp.bfloat16)
+    whole_kv = jnp.sum(lax.all_gather(partial_kv, "ctx"), axis=0).astype(jnp.bfloat16)
     key_step = math.gcd(seq_rows, 512)
 
     def visit(key_block, running):

time: 246 us -> 378 us (1.54)
  the two profiles are of different devices: /device:TPU:8 before, /device:TPU:6 now
where the time goes in v1:
time: 378 us; the launch traced here: 377 us
  waiting for transfers between devices  319 us (84%)
  other arithmetic  24.9 us (7%)
  matrix products  14 us (4%)
  between operations  13.2 us (3%)
    all_gather x1, waiting for transfers between devices, local(): lax.all_gather(partial_kv, 'ctx')  172 us
    all_gather x1, waiting for transfers between devices, local(): lax.all_gather(tokens, 'tensor', axis=0, tiled=True)  50.7 us
    all_gather x1, waiting for transfers between devices, local(): lax.all_gather(attn, 'ctx', axis=0, tiled=True)  50.7 us
    reduce_scatter x1, waiting for transfers between devices, local(): lax.psum_scatter(partial_out.astype(jnp.bfloat16), 'tensor', scatter_dime...  45.3 us
    reduce_sum x1, other arithmetic, local(): jnp.sum(lax.all_gather(partial_kv, 'ctx'), axis=0).astype(jnp.bfloat16)  12.2 us
  transfers between devices with their start and end apart: 4, of which 4 were waited for; matrix products, arithmetic and copies ran while one was open for 1% of the time, Pallas kernels for 0%

profile of v1, /device:TPU:6, one launch (start us, length us, event | category | flops | bytes accessed | tf_op | source)
XLA Modules:
  0.0 377.3 jit_solution(15586471361065709949)
XLA Ops:
  6.5 0.7 all-gather.5.cloned.1.call-update
  7.3 50.7 %all-gather.5.cloned.1.call-done = bf16[2048,512]{1,0:T(8,128)(2,1)} async-done(((bf16[256,512]{1,0:T(8,128)(2,1)}), bf16[2048,512]{1,0:T(8,128)(2,1)}) %all-gather.5.cloned.1.call-update) | async-done | bytes 2097168 | tf_op jit(solution)/shard_map/all_gather | solution.py:81
  58.0 3.6 fusion.22
  63.6 1.2 fusion.19
  64.9 171.9 %all-gather.9.cloned.1.call-done = f32[32768,256]{1,0:T(8,128)} async-done(((f32[2048,256]{1,0:T(8,128)}), f32[32768,256]{1,0:T(8,128)}) %all-gather.9.cloned.1.call-update) | async-done | bytes 33554448 | tf_op jit(solution)/shard_map/all_gather | solution.py:85
  236.8 12.2 %reduce_sum.43 = bf16[2048,256]{1,0:T(8,128)(2,1)S(1)} reduce(f32[16,2048,256]{2,1,0:T(8,128)} %bitcast.66, f32[]{:T(128)} %constant.153.clone.1), dimensions={0}, to_apply=%region_0.0 | reduce | flops 7864320 | bytes 34603012 | tf_op jit(solution)/shard_map/reduce_sum | solution.py:85
  249.0 0.6 copy.21
  249.7 18.4 %while.19 = (s32[]{:T(128)}, f32[128,1,8]{0,2,1:T(8,128)S(1)}, f32[128,1,8]{0,2,1:T(8,128)S(1)}, f32[128,1,8,128]{0,3,2,1:T(8,128)S(1)}, s32[128]{0:T(128)S(1)},...) while((s32[]{:T(128)}, f32[128,1,8]{0,2,1:T(8,128)S(1)}, ...), condition=%wide.region_10.11_spmd.clone, body=%wide.region_3.10_spmd.clone.sunk | while | flops 274742656 | bytes 8730577 | solution.py:92
  249.8 1.2 multiply_add_fusion.2
  251.1 0.9 fusion.28
  252.6 1.7 conditional.3
  254.4 1.2 multiply_add_fusion.2
  255.7 0.9 fusion.28
  257.2 1.7 conditional.3
  259.0 1.2 multiply_add_fusion.2
  260.3 0.9 fusion.28
  261.8 1.7 conditional.3
  263.6 1.2 multiply_add_fusion.2
  264.9 0.9 fusion.28
  266.4 1.7 conditional.3
  268.1 0.8 divide_convert_fusion
  268.9 50.7 %all-gather.7.cloned.1.call-done = bf16[2048,1024]{0,1:T(8,128)(2,1)} async-done(((bf16[128,1024]{0,1:T(8,128)(2,1)}), bf16[2048,1024]{0,1:T(8,128)(2,1)}) %all-gather.7.cloned.1.call-update) | async-done | bytes 4194320 | tf_op jit(solution)/shard_map/all_gather | solution.py:96
  319.6 5.9 %convolution_convert_fusion = bf16[2048,512]{1,0:T(8,128)(2,1)} fusion(bf16[2048,1024]{0,1:T(8,128)(2,1)} %all-gather.7.cloned.1.call-done, bf16[1024,512]{1,0:T(8,128)(2,1)S(1)} %copy-done), kind=kOutput, calls=%fused_computation.30 | convolution fusion | flops 2148532224 | bytes 7340032 | tf_op jit(solution)/shard_map/dot_general | solution.py:95
  325.5 45.3 %reduce-scatter.2.cloned.1.call-done = bf16[256,512]{1,0:T(8,128)(2,1)} async-done(((bf16[2048,512]{1,0:T(8,128)(2,1)}), bf16[256,512]{1,0:T(8,128)(2,1)}) %reduce-scatter.2.cloned.1.call-update) | async-done | bytes 262160 | tf_op jit(solution)/shard_map/reduce_scatter | solution.py:100
  (72 shorter events, 9.3 us)
Async XLA Ops:
  6.5 313.1 %copy-start = (bf16[1024,512]{1,0:T(8,128)(2,1)S(1)}, bf16[1024,512]{1,0:T(8,128)(2,1)}, u32[]{:S(2)}) copy-start(bf16[1024,512]{1,0:T(8,128)(2,1)} %param.15) | copy-start | bytes 3145732
  6.5 51.5 %all-gather.5.cloned.1.call-start = ((), (), s32[]{:S(2)}) async-start(), calls=%async_computation.1 | async-start | bytes 2359296 | tf_op jit(solution)/shard_map/all_gather | solution.py:81
  7.3 229.5 %all-gather.9.cloned.1.call-start = ((), (), s32[]{:S(2)}) async-start(), calls=%async_computation.4 | async-start | bytes 35651584 | tf_op jit(solution)/shard_map/all_gather | solution.py:85
  61.6 0.7 copy-start.3
  61.6 1.0 copy-start.1
  61.6 1.3 copy-start.4
  61.6 2.0 copy-start.2
  61.7 258.0 %all-gather.7.cloned.1.call-start = ((), (), s32[]{:S(2)}) async-start(), calls=%async_computation.2 | async-start | bytes 4456448 | tf_op jit(solution)/shard_map/all_gather | solution.py:96
  268.9 102.0 %reduce-scatter.2.cloned.1.call-start = ((), (), s32[]{:S(2)}) async-start(), calls=%async_computation.3 | async-start | bytes 2359296 | tf_op jit(solution)/shard_map/reduce_scatter | solution.py:100
Sparse Core Ops, SparseCore 0:
  9.4 48.5 all-gather.4
  61.8 174.9 all-gather.8
  269.0 50.5 all-gather.6
  325.7 45.1 reduce-scatter.1
